TPU v7x, 32 devices: a whole 2x2x4 slice. The times are simulated.
32 devices in a mesh: groups: 2 (over x), tok: 16 (over z, y, core).
Axes of the slice: x: 2, y: 2, z: 4, core: 2. Of those that a mesh axis runs over, the one named last changes fastest.
Arguments:
- query_tokens: bfloat16 [3, 4096, 1024], P(None, ('groups', 'tok')), parts along dimension 1, may hold values from -6 to 6
- key_tokens: bfloat16 [3, 4096, 1024], P(None, ('groups', 'tok')), parts along dimension 1, may hold values from -6 to 6
- value_tokens: bfloat16 [3, 4096, 1024], P(None, ('groups', 'tok')), parts along dimension 1, may hold values from -6 to 6
- learn_rates: float32 [3, 4096, 2], P(None, ('groups', 'tok')), parts along dimension 1, may hold values from 0.0009765625 to 0.00390625
- fast_first: bfloat16 [2, 512, 512], P(None, 'tok'), may hold values from -0.25 to 0.25
- fast_third: bfloat16 [2, 512, 512], P(None, 'tok'), may hold values from -0.25 to 0.25
- fast_second: bfloat16 [2, 512, 512], P(None, 'tok'), may hold values from -0.25 to 0.25
- momentum_decay: float32 [2], replicated, may hold values from 0.3 to 0.95
Outputs:
- readout: bfloat16 [3, 4096, 1024], P(None, ('groups', 'tok')), parts along dimension 1
There are 2 independent parts, one for each index of `groups`. A program takes and returns all parts, laid end to end along the dimension named above; an argument that names none is the same for every part. Nothing has to cross between parts.
All inputs are finite; a program needn't handle non-finite values.
Results may differ from a plain program's by a relative error of at most 0.0089.
Values may be sent and summed in bfloat16 or wider, within the bound.
A program may use at most 64 MiB of HBM per device.

v0:
```python
import jax
import jax.numpy as jnp
from jax import lax
from jax.experimental import pallas as pl
from jax.experimental.pallas import tpu as pltpu
from jax.sharding import PartitionSpec as P

MESH = pl.DeviceIdType.MESH


def forward_parts(weights, inputs):
    first, third, second = weights
    length = inputs.shape[0]
    head_count = first.shape[0]
    shaped = inputs.reshape(length, head_count, -1)
    pre_gate = jnp.einsum("thd,hfd->htf", shaped, first, preferred_element_type=jnp.float32)
    pre_up = jnp.einsum("thd,hfd->htf", shaped, third, preferred_element_type=jnp.float32)
    hidden = (jax.nn.silu(pre_gate) * pre_up).astype(jnp.bfloat16)
    return (shaped, pre_gate, pre_up, hidden)


def apply_block(weights, inputs):
    shaped, pre_gate, pre_up, hidden = forward_parts(weights, inputs)
    result = jnp.einsum("htf,hdf->thd", hidden, weights[2], preferred_element_type=jnp.float32)
    return result.reshape(inputs.shape[0], -1).astype(jnp.bfloat16)


def partial_steps(weights, keys, values, rates):
    shaped, pre_gate, pre_up, hidden = forward_parts(weights, keys)
    length = keys.shape[0]
    head_count = weights[0].shape[0]
    scaled = (
        rates[:, :, None] * values.reshape(length, head_count, -1).astype(jnp.float32)
    ).astype(jnp.bfloat16)
    step_second = jnp.einsum("thd,htf->hdf", scaled, hidden, preferred_element_type=jnp.float32)
    back = jnp.einsum("thd,hdf->htf", scaled, weights[2], preferred_element_type=jnp.float32)
    sig_gate = jax.nn.sigmoid(pre_gate)
    d_gate = (back * pre_up * sig_gate * (1.0 + pre_gate * (1.0 - sig_gate))).astype(jnp.bfloat16)
    d_up = (back * pre_gate * sig_gate).astype(jnp.bfloat16)
    step_first = jnp.einsum("htf,thd->hfd", d_gate, shaped, preferred_element_type=jnp.float32)
    step_third = jnp.einsum("htf,thd->hfd", d_up, shaped, preferred_element_type=jnp.float32)
    return (step_first, step_third, step_second)


def renorm(old, moved):
    old_norm = jnp.sqrt(jnp.sum(old * old, axis=-1, keepdims=True) + 1e-06)
    moved_norm = jnp.sqrt(jnp.sum(moved * moved, axis=-1, keepdims=True) + 1e-06)
    return moved * old_norm / moved_norm


def shards(
    query_tokens,
    key_tokens,
    value_tokens,
    learn_rates,
    fast_first,
    fast_third,
    fast_second,
    momentum_decay,
):
    owned_zero = jnp.stack([fast_first, fast_third, fast_second])
    full_zero = lax.all_gather(owned_zero, "tok", axis=2, tiled=True)
    terms_zero = partial_steps(full_zero, key_tokens[0], value_tokens[0], learn_rates[0])
    terms_one = partial_steps(full_zero, key_tokens[1], value_tokens[1], learn_rates[1])
    step_zero = lax.psum_scatter(
        jnp.stack(terms_zero).astype(jnp.bfloat16), "tok", scatter_dimension=2, tiled=True
    ).astype(jnp.float32)
    step_one = lax.psum_scatter(
        jnp.stack(terms_one).astype(jnp.bfloat16), "tok", scatter_dimension=2, tiled=True
    ).astype(jnp.float32)
    out_zero = apply_block(full_zero, query_tokens[0])
    decay = momentum_decay[None, :, None, None]
    weights_zero = owned_zero.astype(jnp.float32)
    weights_one = renorm(weights_zero, weights_zero + step_zero)
    full_one = lax.all_gather(weights_one.astype(jnp.bfloat16), "tok", axis=2, tiled=True)
    weights_two = renorm(weights_one, weights_one + decay * step_zero + step_one)
    full_two = lax.all_gather(weights_two.astype(jnp.bfloat16), "tok", axis=2, tiled=True)
    out_one = apply_block(full_one, query_tokens[1])
    out_two = apply_block(full_two, query_tokens[2])
    return jnp.stack([out_zero, out_one, out_two])


def dot_nt(a, b):
    return lax.dot_general(a, b, (((1,), (1,)), ((), ())), preferred_element_type=jnp.float32)


def dot_nn(a, b):
    return lax.dot_general(a, b, (((1,), (0,)), ((), ())), preferred_element_type=jnp.float32)


def dot_tn(a, b):
    return lax.dot_general(a, b, (((0,), (0,)), ((), ())), preferred_element_type=jnp.float32)


def kernel(
    query_ref,
    key_ref,
    value_ref,
    rate_ref,
    first_ref,
    third_ref,
    second_ref,
    decay_ref,
    out_ref,
    queries,
    keys,
    values,
    rates,
    full,
    part,
    core_out,
    core_in,
    side_out,
    side_in,
    far_out,
    far_in,
    step_own,
    weight_own,
    result,
    gates,
    ups,
    hiddens,
    swap_send,
    swap_recv,
    local_sem,
    gather_send,
    gather_recv,
    share_send,
    share_recv,
    sum_send,
    sum_recv,
    out_send,
    out_recv,
    out_local,
):
    index = lax.axis_index("tok")
    core = index % 2
    lane = (index // 2) % 2
    head = (index // 4) % 2
    pair = index // 8
    group = lax.axis_index("groups")
    across = {"groups": 1 - group}
    partner = {"tok": index + 1 - 2 * core}
    beside = {"tok": index + 2 - 4 * lane}
    mate = {"tok": index + 4 - 8 * head}
    beyond = {"tok": index + 8 - 16 * pair}
    rows = first_ref.shape[1]
    tokens = key_ref.shape[1]
    width = first_ref.shape[2]
    hidden_units = 16 * rows

    barrier = pltpu.get_barrier_semaphore()
    for other in (partner, beside, mate, beyond, across):
        pl.semaphore_signal(barrier, inc=1, device_id=other, device_id_type=MESH)
    pl.semaphore_wait(barrier, 5)

    sent = []

    def push(src, dst, send_sem, recv_sem, to):
        return pltpu.make_async_remote_copy(
            src_ref=src,
            dst_ref=dst,
            send_sem=send_sem,
            recv_sem=recv_sem,
            device_id=to,
            device_id_type=MESH,
        )

    def go(copy):
        copy.start()
        sent.append(copy)

    mine = pl.ds(pl.multiple_of(head * width, width), width)
    theirs = pl.ds(pl.multiple_of((1 - head) * width, width), width)
    slot = pl.ds(pl.multiple_of(head * tokens, tokens), tokens)
    other_slot = pl.ds(pl.multiple_of((1 - head) * tokens, tokens), tokens)

    pairs = []
    for m, ref in enumerate((first_ref, third_ref, second_ref)):
        pairs.append((ref.at[1 - head], ref.at[head], full.at[0, m, pair, head, lane, core]))
    for b in range(2):
        pairs.append((key_ref.at[b, :, theirs], key_ref.at[b, :, mine], keys.at[b, slot, :]))
        pairs.append((value_ref.at[b, :, theirs], value_ref.at[b, :, mine], values.at[b, slot, :]))
        pairs.append((rate_ref.at[b], rate_ref.at[b], rates.at[b, :, slot]))
    for b in range(3):
        pairs.append((query_ref.at[b, :, theirs], query_ref.at[b, :, mine], queries.at[b, slot, :]))
    swaps = {}
    locals_ = {}

    def swap(first, last):
        for n in range(first, last):
            away, here, target = pairs[n]
            swaps[n] = push(away, target, swap_send.at[n], swap_recv.at[n], mate)
            swaps[n].start()
            locals_[n] = pltpu.make_async_copy(here, target, local_sem.at[n])
            locals_[n].start()

    def ready(n):
        swaps[n].wait_recv()
        locals_[n].wait()

    def block_of(k, m, p, q):
        return full.at[k, m, p, :, q, core]

    def gather_copy(k, m, n):
        p, q = (
            (pair, lane),
            (pair, lane),
            (1 - pair, lane),
            (pair, lane),
            (1 - pair, lane),
            (pair, 1 - lane),
            (1 - pair, 1 - lane),
        )[n]
        span = block_of(k, m, p, q)
        to = (beyond, beside, beside, partner, partner, partner, partner)[n]
        return push(span, span, gather_send.at[k, m, n], gather_recv.at[k, m, n], to)

    share = pl.ds(pl.multiple_of(group * (width // 2), width // 2), width // 2)

    def share_copy(m, n):
        copy_from, to = (
            ((pair, lane), beyond),
            ((pair, lane), beside),
            ((1 - pair, lane), beside),
            ((1 - pair, lane), across),
            ((pair, 1 - lane), across),
            ((1 - pair, 1 - lane), across),
        )[n]
        span = full.at[0, m, copy_from[0], :, copy_from[1], core, :, share]
        return push(span, span, share_send.at[m, n], share_recv.at[m, n], to)

    def share_all():
        for m in range(3):
            share_copy(m, 0).wait_recv()
            go(share_copy(m, 2))
            go(share_copy(m, 3))
            share_copy(m, 1).wait_recv()
            go(share_copy(m, 4))
        for m in range(3):
            share_copy(m, 3).wait_recv()
            go(gather_copy(0, m, 4))
            share_copy(m, 2).wait_recv()
            go(share_copy(m, 5))
            share_copy(m, 4).wait_recv()
            go(gather_copy(0, m, 5))
        for m in range(3):
            share_copy(m, 5).wait_recv()
            go(gather_copy(0, m, 6))

    def gather_own(k, m):
        for n in (0, 1, 3):
            go(gather_copy(k, m, n))

    def gather_beyond(k, m):
        gather_copy(k, m, 0).wait_recv()
        go(gather_copy(k, m, 2))
        go(gather_copy(k, m, 4))

    def gather_beside(k, m, n):
        gather_copy(k, m, n).wait_recv()
        go(gather_copy(k, m, n + 4))

    def gather_end(k, m):
        for n in range(3, 7):
            gather_copy(k, m, n).wait_recv()

    def core_copy(t):
        return push(
            core_out.at[t], core_in.at[t], sum_send.at[t, 0], sum_recv.at[t, 0], partner
        )

    def side_copy(t, p, n):
        return push(
            side_out.at[t, p], side_in.at[t, p], sum_send.at[t, n], sum_recv.at[t, n], beside
        )

    def far_copy(t):
        return push(far_out.at[t], far_in.at[t], sum_send.at[t, 3], sum_recv.at[t, 3], beyond)

    def core_start(t):
        core_out[t] = part[t, :, :, :, 1 - core].astype(jnp.bfloat16)
        go(core_copy(t))

    def core_sum(t, p, q):
        return part[t, p, :, q, core] + core_in[t, p, :, q].astype(jnp.float32)

    def side_start(t):
        core_copy(t).wait_recv()
        for n, p in ((1, 1 - pair), (2, pair)):
            side_out[t, p] = core_sum(t, p, 1 - lane).astype(jnp.bfloat16)
            go(side_copy(t, p, n))

    def far_start(t):
        p = 1 - pair
        side_copy(t, p, 1).wait_recv()
        far_out[t] = (core_sum(t, p, lane) + side_in[t, p].astype(jnp.float32)).astype(
            jnp.bfloat16
        )
        go(far_copy(t))

    def total_of(t):
        side_copy(t, pair, 2).wait_recv()
        near = core_sum(t, pair, lane) + side_in[t, pair].astype(jnp.float32)
        far_copy(t).wait_recv()
        return near + far_in[t].astype(jnp.float32)

    order = (2, 0, 1)

    def whole(k, m):
        return full[k, m].reshape(hidden_units, width)

    def forward(k, x):
        gate = dot_nt(x, whole(k, 0))
        up = dot_nt(x, whole(k, 1))
        sig = jax.nn.sigmoid(gate)
        return gate, up, sig, (gate * sig * up).astype(jnp.bfloat16)

    def keys_forward(j):
        gate, up, sig, hidden = forward(0, keys[j])
        gates[...] = gate
        ups[...] = up
        hiddens[...] = hidden

    def steps(j):
        row = jnp.where(head == 0, rates[j, 0:1, :], rates[j, 1:2, :])
        rate = jnp.transpose(jnp.broadcast_to(row, (128, row.shape[1])))[:, 0:1]
        scaled = (rate * values[j].astype(jnp.float32)).astype(jnp.bfloat16)
        part[3 * j + 2] = dot_tn(scaled, hiddens[...]).reshape(part.shape[1:])
        core_start(3 * j + 2)
        back = dot_nn(scaled, whole(0, 2))
        gate = gates[...]
        sig = jax.nn.sigmoid(gate)
        x = keys[j]
        d_gate = (back * ups[...] * sig * (1.0 + gate * (1.0 - sig))).astype(jnp.bfloat16)
        part[3 * j] = dot_tn(d_gate, x).reshape(part.shape[1:])
        core_start(3 * j)
        d_up = (back * gate * sig).astype(jnp.bfloat16)
        part[3 * j + 1] = dot_tn(d_up, x).reshape(part.shape[1:])
        core_start(3 * j + 1)

    outs = []

    def read_hidden(k):
        gate, up, sig, hidden = forward(k, queries[k])
        hiddens[...] = hidden

    def read_out(k):
        result[k] = dot_nt(hiddens[...], whole(k, 2)).astype(jnp.bfloat16)
        away = push(
            result.at[k, other_slot, :],
            out_ref.at[k, :, mine],
            out_send.at[k],
            out_recv.at[k],
            mate,
        )
        away.start()
        here = pltpu.make_async_copy(
            result.at[k, slot, :], out_ref.at[k, :, mine], out_local.at[k]
        )
        here.start()
        outs.append((away, here))

    swap(0, 3)
    for m in range(3):
        ready(m)
        go(share_copy(m, 0))
        go(share_copy(m, 1))
        go(gather_copy(0, m, 3))
    swap(3, 9)
    share_all()
    for m in range(3):
        gather_end(0, m)
    for n in range(3, 6):
        ready(n)
    keys_forward(0)
    steps(0)
    for m in order:
        side_start(m)
    for n in range(6, 9):
        ready(n)
    keys_forward(1)
    steps(1)
    for m in order:
        far_start(m)
        side_start(3 + m)
    swap(9, 10)
    for m in order:
        moment = total_of(m)
        step_own[m] = moment
        old = full[0, m, pair, :, lane, core].astype(jnp.float32)
        fresh = renorm(old, old + moment)
        weight_own[m] = fresh
        full[1, m, pair, :, lane, core] = fresh.astype(jnp.bfloat16)
        gather_own(1, m)
    decay = decay_ref[head]
    for m in order:
        far_start(3 + m)
    swap(10, 11)
    ready(9)
    read_hidden(0)
    read_out(0)
    for m in order:
        gather_beyond(1, m)
        gather_beside(1, m, 1)
    for m in order:
        moment = decay * step_own[m] + total_of(3 + m)
        old = weight_own[m]
        fresh = renorm(old, old + moment)
        full[2, m, pair, :, lane, core] = fresh.astype(jnp.bfloat16)
        gather_own(2, m)
    swap(11, 12)
    for m in order:
        gather_beside(1, m, 2)
    for m in order:
        gather_beyond(2, m)
        gather_beside(2, m, 1)
    for m in range(3):
        gather_end(1, m)
    ready(10)
    read_hidden(1)
    read_out(1)
    ready(11)
    for m in order:
        gather_beside(2, m, 2)
    gather_end(2, 2)
    gather_end(2, 0)
    gates[...] = dot_nt(queries[2], whole(2, 0))
    gather_end(2, 1)
    gate = gates[...]
    up = dot_nt(queries[2], whole(2, 1))
    hiddens[...] = (gate * jax.nn.sigmoid(gate) * up).astype(jnp.bfloat16)
    read_out(2)

    for n in range(len(pairs)):
        swaps[n].wait_send()
    for copy in sent:
        copy.wait_send()
    for away, here in outs:
        here.wait()
        away.wait()


def fused_shards(query, key, value, rate, first, third, second, decay):
    blocks, tokens, features = query.shape
    heads, rows, width = first.shape
    hidden = 16 * rows
    span = 2 * tokens
    anywhere = pl.BlockSpec(memory_space=pl.ANY)
    dma = pltpu.SemaphoreType.DMA
    low, wide = jnp.bfloat16, jnp.float32
    return pl.pallas_call(
        kernel,
        out_shape=jax.ShapeDtypeStruct(query.shape, low),
        in_specs=[anywhere] * 7 + [pl.BlockSpec(memory_space=pltpu.SMEM)],
        out_specs=anywhere,
        scratch_shapes=[
            pltpu.VMEM((3, span, width), low),
            pltpu.VMEM((2, span, width), low),
            pltpu.VMEM((2, span, width), low),
            pltpu.VMEM((2, heads, span), wide),
            pltpu.VMEM((3, 3, 2, 2, 2, 2, rows, width), low),
            pltpu.VMEM((6, 2, 2, 2, 2, rows, width), wide),
            pltpu.VMEM((6, 2, 2, 2, rows, width), low),
            pltpu.VMEM((6, 2, 2, 2, rows, width), low),
            pltpu.VMEM((6, 2, 2, rows, width), low),
            pltpu.VMEM((6, 2, 2, rows, width), low),
            pltpu.VMEM((6, 2, rows, width), low),
            pltpu.VMEM((6, 2, rows, width), low),
            pltpu.VMEM((3, 2, rows, width), wide),
            pltpu.VMEM((3, 2, rows, width), wide),
            pltpu.VMEM((3, span, width), low),
            pltpu.VMEM((span, hidden), wide),
            pltpu.VMEM((span, hidden), wide),
            pltpu.VMEM((span, hidden), low),
            dma((12,)),
            dma((12,)),
            dma((12,)),
            dma((3, 3, 7)),
            dma((3, 3, 7)),
            dma((3, 6)),
            dma((3, 6)),
            dma((6, 4)),
            dma((6, 4)),
            dma((3,)),
            dma((3,)),
            dma((3,)),
        ],
        compiler_params=pltpu.CompilerParams(
            collective_id=0, has_side_effects=True, vmem_limit_bytes=60 * 1024 * 1024
        ),
    )(query, key, value, jnp.swapaxes(rate, 1, 2), first, third, second, decay)


def solution(mesh):
    placed = (
        P(None, ("groups", "tok"), None),
        P(None, ("groups", "tok"), None),
        P(None, ("groups", "tok"), None),
        P(None, ("groups", "tok"), None),
        P(None, "tok", None),
        P(None, "tok", None),
        P(None, "tok", None),
        P(),
    )
    chips = mesh.shape["tok"] // 2

    def body(*arrays):
        rows = arrays[4].shape[1]
        if rows % 16 or chips != 8 or arrays[4].shape[0] != 2 or mesh.shape["groups"] != 2:
            return shards(*arrays)
        return fused_shards(*arrays)

    return jax.shard_map(
        body,
        mesh=mesh,
        in_specs=placed,
        out_specs=P(None, ("groups", "tok"), None),
        check_vma=False,
    )
```

profile of v0, /device:TPU:0, one launch (start us, length us, event | category | flops | bytes accessed | tf_op | source)
XLA Modules:
  0.0 75.0 jit_solution(15360866596358594528)
XLA Ops:
  0.0 72.9 %shard_map.82 = bf16[3,128,1024]{2,1,0:T(8,128)(2,1)} custom-call(bf16[3,128,1024]{2,1,0:T(8,128)(2,1)} %query_ref.1, bf16[3,128,1024]{2,1,0:T(8,128)(2,1)} %key_ref.1, bf16[3,128,1024]{2,1,0:T(8,128)(2,1)} %value_ref.1, f32[3,2,128]{2,1,0:T(2,128)} %bitcast.1, bf16[2,32,512]{2,1,0:T(8,128)(2,1)} %first_ref.1, bf16[2,32,512]{2,1,0:T(8,128)(2,1)} %third_ref.1, ...), custom_call_target="tpu_custom_call" | custom-call | tf_op jit(solution)/shard_map/pallas_call | solution.py:452
  73.0 2.1 %copy.10 = bf16[3,128,1024]{2,1,0:T(8,128)(2,1)} copy(bf16[3,128,1024]{2,1,0:T(8,128)(2,1)} %shard_map.82) | data formatting | bytes 1572864
where the time goes:
time: 75.2 us; the launch traced here: 75 us
  Pallas kernels  72.9 us (97%)
  local copies, waits for them, and re-layouts  2.06 us (3%)
    pallas_call x1, Pallas kernels, fused_shards(): pl.pallas_call(kernel, out_shape=jax.ShapeDtypeStruct(query.shape, low),...  72.9 us
    unnamed x1, local copies, waits for them, and re-layouts  2.06 us

commit v1 on v0

--- a/solution.py
+++ b/solution.py
@@ -125,8 +125,9 @@
     local_sem,
     gather_send,
     gather_recv,
-    share_send,
-    share_recv,
+    first_send,
+    first_recv,
+    first_local,
     sum_send,
     sum_recv,
     out_send,
@@ -144,15 +145,18 @@
     beside = {"tok": index + 2 - 4 * lane}
     mate = {"tok": index + 4 - 8 * head}
     beyond = {"tok": index + 8 - 16 * pair}
+    crossed = {"tok": index + 12 - 8 * head - 16 * pair}
+    corner = {"groups": 1 - group, "tok": index + 2 - 4 * lane}
     rows = first_ref.shape[1]
     tokens = key_ref.shape[1]
     width = first_ref.shape[2]
     hidden_units = 16 * rows
 
     barrier = pltpu.get_barrier_semaphore()
-    for other in (partner, beside, mate, beyond, across):
+    others = (crossed, beyond, corner, mate, beside, across, partner)
+    for other in others:
         pl.semaphore_signal(barrier, inc=1, device_id=other, device_id_type=MESH)
-    pl.semaphore_wait(barrier, 5)
+    pl.semaphore_wait(barrier, len(others))
 
     sent = []
 
@@ -176,8 +180,6 @@
     other_slot = pl.ds(pl.multiple_of((1 - head) * tokens, tokens), tokens)
 
     pairs = []
-    for m, ref in enumerate((first_ref, third_ref, second_ref)):
-        pairs.append((ref.at[1 - head], ref.at[head], full.at[0, m, pair, head, lane, core]))
     for b in range(2):
         pairs.append((key_ref.at[b, :, theirs], key_ref.at[b, :, mine], keys.at[b, slot, :]))
         pairs.append((value_ref.at[b, :, theirs], value_ref.at[b, :, mine], values.at[b, slot, :]))
@@ -214,39 +216,69 @@
         )[n]
         span = block_of(k, m, p, q)
         to = (beyond, beside, beside, partner, partner, partner, partner)[n]
-        return push(span, span, gather_send.at[k, m, n], gather_recv.at[k, m, n], to)
+        return push(span, span, gather_send.at[k - 1, m, n], gather_recv.at[k - 1, m, n], to)
 
     share = pl.ds(pl.multiple_of(group * (width // 2), width // 2), width // 2)
-
-    def share_copy(m, n):
-        copy_from, to = (
-            ((pair, lane), beyond),
-            ((pair, lane), beside),
-            ((1 - pair, lane), beside),
-            ((1 - pair, lane), across),
-            ((pair, 1 - lane), across),
-            ((1 - pair, 1 - lane), across),
+    initial = (first_ref, third_ref, second_ref)
+
+    def first_copy(m, n):
+        ref = initial[m]
+        own = full.at[0, m, pair, head, lane, core]
+        near = full.at[0, m, pair, 1 - head, lane, core]
+        wide = full.at[0, m, 1 - pair, :, lane, core, :, share]
+        src, dst, to = (
+            (ref.at[1 - head], own, mate),
+            (ref.at[head, :, share], own.at[:, share], beyond),
+            (ref.at[1 - head, :, share], own.at[:, share], crossed),
+            (ref.at[head], own, beside),
+            (ref.at[head], own, partner),
+            (near, near, beside),
+            (near, near, partner),
+            (wide, wide, beside),
+            (wide, wide, across),
+            (wide, wide, corner),
+            (block_of(0, m, pair, 1 - lane),) * 2 + (partner,),
+            (block_of(0, m, 1 - pair, lane),) * 2 + (partner,),
+            (block_of(0, m, 1 - pair, 1 - lane),) * 2 + (partner,),
         )[n]
-        span = full.at[0, m, copy_from[0], :, copy_from[1], core, :, share]
-        return push(span, span, share_send.at[m, n], share_recv.at[m, n], to)
-
-    def share_all():
+        return push(src, dst, first_send.at[m, n], first_recv.at[m, n], to)
+
+    def first_here(m):
+        return pltpu.make_async_copy(
+            initial[m].at[head], full.at[0, m, pair, head, lane, core], first_local.at[m]
+        )
+
+    def first_start():
         for m in range(3):
-            share_copy(m, 0).wait_recv()
-            go(share_copy(m, 2))
-            go(share_copy(m, 3))
-            share_copy(m, 1).wait_recv()
-            go(share_copy(m, 4))
+            for n in (2, 1, 0, 3, 4):
+                go(first_copy(m, n))
+            first_here(m).start()
+
+    def first_spread():
         for m in range(3):
-            share_copy(m, 3).wait_recv()
-            go(gather_copy(0, m, 4))
-            share_copy(m, 2).wait_recv()
-            go(share_copy(m, 5))
-            share_copy(m, 4).wait_recv()
-            go(gather_copy(0, m, 5))
+            first_copy(m, 0).wait_recv()
+            go(first_copy(m, 5))
+            go(first_copy(m, 6))
         for m in range(3):
-            share_copy(m, 5).wait_recv()
-            go(gather_copy(0, m, 6))
+            first_copy(m, 2).wait_recv()
+            first_copy(m, 1).wait_recv()
+            for n in (7, 9, 8):
+                go(first_copy(m, n))
+        for m in range(3):
+            first_copy(m, 3).wait_recv()
+            first_copy(m, 5).wait_recv()
+            go(first_copy(m, 10))
+        for m in range(3):
+            first_copy(m, 8).wait_recv()
+            go(first_copy(m, 11))
+            first_copy(m, 7).wait_recv()
+            first_copy(m, 9).wait_recv()
+            go(first_copy(m, 12))
+
+    def first_end(m):
+        first_here(m).wait()
+        for n in (4, 6, 10, 11, 12):
+            first_copy(m, n).wait_recv()
 
     def gather_own(k, m):
         for n in (0, 1, 3):
@@ -285,11 +317,14 @@
     def core_sum(t, p, q):
         return part[t, p, :, q, core] + core_in[t, p, :, q].astype(jnp.float32)
 
-    def side_start(t):
-        core_copy(t).wait_recv()
-        for n, p in ((1, 1 - pair), (2, pair)):
-            side_out[t, p] = core_sum(t, p, 1 - lane).astype(jnp.bfloat16)
-            go(side_copy(t, p, n))
+    def side_start(ts):
+        for n in (1, 2):
+            for t in ts:
+                if n == 1:
+                    core_copy(t).wait_recv()
+                p = 1 - pair if n == 1 else pair
+                side_out[t, p] = core_sum(t, p, 1 - lane).astype(jnp.bfloat16)
+                go(side_copy(t, p, n))
 
     def far_start(t):
         p = 1 - pair
@@ -328,6 +363,8 @@
         scaled = (rate * values[j].astype(jnp.float32)).astype(jnp.bfloat16)
         part[3 * j + 2] = dot_tn(scaled, hiddens[...]).reshape(part.shape[1:])
         core_start(3 * j + 2)
+        if j == 0:
+            first_end(2)
         back = dot_nn(scaled, whole(0, 2))
         gate = gates[...]
         sig = jax.nn.sigmoid(gate)
@@ -361,30 +398,24 @@
         here.start()
         outs.append((away, here))
 
-    swap(0, 3)
-    for m in range(3):
-        ready(m)
-        go(share_copy(m, 0))
-        go(share_copy(m, 1))
-        go(gather_copy(0, m, 3))
-    swap(3, 9)
-    share_all()
-    for m in range(3):
-        gather_end(0, m)
-    for n in range(3, 6):
+    first_start()
+    swap(0, 6)
+    first_spread()
+    for m in range(2):
+        first_end(m)
+    for n in range(0, 3):
         ready(n)
     keys_forward(0)
     steps(0)
-    for m in order:
-        side_start(m)
-    for n in range(6, 9):
+    side_start(order)
+    for n in range(3, 6):
         ready(n)
     keys_forward(1)
     steps(1)
     for m in order:
         far_start(m)
-        side_start(3 + m)
-    swap(9, 10)
+    side_start([3 + m for m in order])
+    swap(6, 7)
     for m in order:
         moment = total_of(m)
         step_own[m] = moment
@@ -396,20 +427,20 @@
     decay = decay_ref[head]
     for m in order:
         far_start(3 + m)
-    swap(10, 11)
-    ready(9)
+    swap(7, 8)
+    for m in order:
+        gather_beyond(1, m)
+        gather_beside(1, m, 1)
+    ready(6)
     read_hidden(0)
     read_out(0)
-    for m in order:
-        gather_beyond(1, m)
-        gather_beside(1, m, 1)
     for m in order:
         moment = decay * step_own[m] + total_of(3 + m)
         old = weight_own[m]
         fresh = renorm(old, old + moment)
         full[2, m, pair, :, lane, core] = fresh.astype(jnp.bfloat16)
         gather_own(2, m)
-    swap(11, 12)
+    swap(8, 9)
     for m in order:
         gather_beside(1, m, 2)
     for m in order:
@@ -417,10 +448,10 @@
         gather_beside(2, m, 1)
     for m in range(3):
         gather_end(1, m)
-    ready(10)
+    ready(7)
     read_hidden(1)
     read_out(1)
-    ready(11)
+    ready(8)
     for m in order:
         gather_beside(2, m, 2)
     gather_end(2, 2)
@@ -473,13 +504,14 @@
             pltpu.VMEM((span, hidden), wide),
             pltpu.VMEM((span, hidden), wide),
             pltpu.VMEM((span, hidden), low),
-            dma((12,)),
-            dma((12,)),
-            dma((12,)),
-            dma((3, 3, 7)),
-            dma((3, 3, 7)),
-            dma((3, 6)),
-            dma((3, 6)),
+            dma((9,)),
+            dma((9,)),
+            dma((9,)),
+            dma((2, 3, 7)),
+            dma((2, 3, 7)),
+            dma((3, 13)),
+            dma((3, 13)),
+            dma((3,)),
             dma((6, 4)),
             dma((6, 4)),
             dma((3,)),

time: 75.2 us -> 73.3 us (0.975); the launches traced: 75 us -> 72.3 us
  Pallas kernels: 72.9 us -> 70.2 us
    pallas_call x1, Pallas kernels: 72.9 us -> 70.2 us  [fused_shards(): pl.pallas_call(kernel, out_shape=jax.ShapeDtypeStruct(query.shape, low),...]
where the time goes in v1:
time: 73.3 us; the launch traced here: 72.3 us
  Pallas kernels  70.2 us (96%)
  local copies, waits for them, and re-layouts  2.06 us (3%)
    pallas_call x1, Pallas kernels, fused_shards(): pl.pallas_call(kernel, out_shape=jax.ShapeDtypeStruct(query.shape, low),...  70.2 us
    unnamed x1, local copies, waits for them, and re-layouts  2.06 us

profile of v1, /device:TPU:0, one launch (start us, length us, event | category | flops | bytes accessed | tf_op | source)
XLA Modules:
  0.0 72.3 jit_solution(2243217349193595253)
XLA Ops:
  0.0 70.2 %shard_map.82 = bf16[3,128,1024]{2,1,0:T(8,128)(2,1)} custom-call(bf16[3,128,1024]{2,1,0:T(8,128)(2,1)} %query_ref.1, bf16[3,128,1024]{2,1,0:T(8,128)(2,1)} %key_ref.1, bf16[3,128,1024]{2,1,0:T(8,128)(2,1)} %value_ref.1, f32[3,2,128]{2,1,0:T(2,128)} %bitcast.1, bf16[2,32,512]{2,1,0:T(8,128)(2,1)} %first_ref.1, bf16[2,32,512]{2,1,0:T(8,128)(2,1)} %third_ref.1, ...), custom_call_target="tpu_custom_call" | custom-call | tf_op jit(solution)/shard_map/pallas_call | solution.py:483
  70.2 2.1 %copy.10 = bf16[3,128,1024]{2,1,0:T(8,128)(2,1)} copy(bf16[3,128,1024]{2,1,0:T(8,128)(2,1)} %shard_map.82) | data formatting | bytes 1572864

commit v2 on v1

--- a/solution.py
+++ b/solution.py
@@ -128,6 +128,7 @@
     first_send,
     first_recv,
     first_local,
+    rows_here,
     sum_send,
     sum_recv,
     out_send,
@@ -152,6 +153,9 @@
     width = first_ref.shape[2]
     hidden_units = 16 * rows
 
+    for m, ref in enumerate((first_ref, third_ref, second_ref)):
+        pltpu.make_async_copy(ref, rows_here.at[m], first_local.at[m]).start()
+
     barrier = pltpu.get_barrier_semaphore()
     others = (crossed, beyond, corner, mate, beside, across, partner)
     for other in others:
@@ -219,24 +223,25 @@
         return push(span, span, gather_send.at[k - 1, m, n], gather_recv.at[k - 1, m, n], to)
 
     share = pl.ds(pl.multiple_of(group * (width // 2), width // 2), width // 2)
-    initial = (first_ref, third_ref, second_ref)
 
     def first_copy(m, n):
-        ref = initial[m]
+        ref = rows_here.at[m]
         own = full.at[0, m, pair, head, lane, core]
         near = full.at[0, m, pair, 1 - head, lane, core]
         wide = full.at[0, m, 1 - pair, :, lane, core, :, share]
         src, dst, to = (
-            (ref.at[1 - head], own, mate),
+            (ref.at[1 - head, :, share], own.at[:, share], mate),
             (ref.at[head, :, share], own.at[:, share], beyond),
             (ref.at[1 - head, :, share], own.at[:, share], crossed),
             (ref.at[head], own, beside),
             (ref.at[head], own, partner),
-            (near, near, beside),
-            (near, near, partner),
+            (near.at[:, share], near.at[:, share], beside),
+            (near.at[:, share], near.at[:, share], across),
             (wide, wide, beside),
             (wide, wide, across),
             (wide, wide, corner),
+            (near.at[:, share], near.at[:, share], corner),
+            (near, near, partner),
             (block_of(0, m, pair, 1 - lane),) * 2 + (partner,),
             (block_of(0, m, 1 - pair, lane),) * 2 + (partner,),
             (block_of(0, m, 1 - pair, 1 - lane),) * 2 + (partner,),
@@ -245,10 +250,12 @@
 
     def first_here(m):
         return pltpu.make_async_copy(
-            initial[m].at[head], full.at[0, m, pair, head, lane, core], first_local.at[m]
+            rows_here.at[m, head], full.at[0, m, pair, head, lane, core], first_local.at[m]
         )
 
     def first_start():
+        for m, ref in enumerate((first_ref, third_ref, second_ref)):
+            pltpu.make_async_copy(ref, rows_here.at[m], first_local.at[m]).wait()
         for m in range(3):
             for n in (2, 1, 0, 3, 4):
                 go(first_copy(m, n))
@@ -257,27 +264,29 @@
     def first_spread():
         for m in range(3):
             first_copy(m, 0).wait_recv()
-            go(first_copy(m, 5))
-            go(first_copy(m, 6))
+            for n in (5, 10, 6):
+                go(first_copy(m, n))
         for m in range(3):
             first_copy(m, 2).wait_recv()
             first_copy(m, 1).wait_recv()
             for n in (7, 9, 8):
                 go(first_copy(m, n))
         for m in range(3):
-            first_copy(m, 3).wait_recv()
-            first_copy(m, 5).wait_recv()
-            go(first_copy(m, 10))
+            first_copy(m, 6).wait_recv()
+            go(first_copy(m, 11))
+            for n in (3, 5, 10):
+                first_copy(m, n).wait_recv()
+            go(first_copy(m, 12))
         for m in range(3):
             first_copy(m, 8).wait_recv()
-            go(first_copy(m, 11))
+            go(first_copy(m, 13))
             first_copy(m, 7).wait_recv()
             first_copy(m, 9).wait_recv()
-            go(first_copy(m, 12))
+            go(first_copy(m, 14))
 
     def first_end(m):
         first_here(m).wait()
-        for n in (4, 6, 10, 11, 12):
+        for n in (4, 11, 12, 13, 14):
             first_copy(m, n).wait_recv()
 
     def gather_own(k, m):
@@ -384,6 +393,10 @@
 
     def read_out(k):
         result[k] = dot_nt(hiddens[...], whole(k, 2)).astype(jnp.bfloat16)
+        send_out(k)
+        keep_out(k)
+
+    def send_out(k):
         away = push(
             result.at[k, other_slot, :],
             out_ref.at[k, :, mine],
@@ -392,11 +405,14 @@
             mate,
         )
         away.start()
+        outs.append(away)
+
+    def keep_out(k):
         here = pltpu.make_async_copy(
             result.at[k, slot, :], out_ref.at[k, :, mine], out_local.at[k]
         )
         here.start()
-        outs.append((away, here))
+        outs.append(here)
 
     first_start()
     swap(0, 6)
@@ -458,18 +474,21 @@
     gather_end(2, 0)
     gates[...] = dot_nt(queries[2], whole(2, 0))
     gather_end(2, 1)
-    gate = gates[...]
-    up = dot_nt(queries[2], whole(2, 1))
-    hiddens[...] = (gate * jax.nn.sigmoid(gate) * up).astype(jnp.bfloat16)
-    read_out(2)
+    for place in (other_slot, slot):
+        gate = gates[place, :]
+        up = dot_nt(queries[2, place, :], whole(2, 1))
+        hidden = (gate * jax.nn.sigmoid(gate) * up).astype(jnp.bfloat16)
+        result[2, place, :] = dot_nt(hidden, whole(2, 2)).astype(jnp.bfloat16)
+        if place is other_slot:
+            send_out(2)
+    keep_out(2)
 
     for n in range(len(pairs)):
         swaps[n].wait_send()
     for copy in sent:
         copy.wait_send()
-    for away, here in outs:
-        here.wait()
-        away.wait()
+    for copy in outs:
+        copy.wait()
 
 
 def fused_shards(query, key, value, rate, first, third, second, decay):
@@ -482,9 +501,9 @@
     low, wide = jnp.bfloat16, jnp.float32
     return pl.pallas_call(
         kernel,
-        out_shape=jax.ShapeDtypeStruct(query.shape, low),
+        out_shape=pltpu.VMEM(query.shape, low),
         in_specs=[anywhere] * 7 + [pl.BlockSpec(memory_space=pltpu.SMEM)],
-        out_specs=anywhere,
+        out_specs=pl.BlockSpec(memory_space=pltpu.VMEM),
         scratch_shapes=[
             pltpu.VMEM((3, span, width), low),
             pltpu.VMEM((2, span, width), low),
@@ -509,9 +528,10 @@
             dma((9,)),
             dma((2, 3, 7)),
             dma((2, 3, 7)),
-            dma((3, 13)),
-            dma((3, 13)),
+            dma((3, 15)),
+            dma((3, 15)),
             dma((3,)),
+            pltpu.VMEM((3, heads, rows, width), low),
             dma((6, 4)),
             dma((6, 4)),
             dma((3,)),

time: 73.3 us -> 71.9 us (0.981); the launches traced: 72.3 us -> 71.8 us
  local copies, waits for them, and re-layouts: 2.06 us -> 0.88 us
    unnamed x1, local copies, waits for them, and re-layouts: 2.06 us -> 0.88 us
where the time goes in v2:
time: 71.9 us; the launch traced here: 71.8 us
  Pallas kernels  70.9 us (99%)
  local copies, waits for them, and re-layouts  0.88 us (1%)
    pallas_call x1, Pallas kernels, fused_shards(): pl.pallas_call(kernel, out_shape=pltpu.VMEM(query.shape, low), in_specs=[...  70.9 us

profile of v2, /device:TPU:0, one launch (start us, length us, event | category | flops | bytes accessed | tf_op | source)
XLA Modules:
  0.0 71.8 jit_solution(3629435339965917787)
XLA Ops:
  0.0 70.9 %shard_map.82 = bf16[3,128,1024]{2,1,0:T(8,128)(2,1)S(1)} custom-call(bf16[3,128,1024]{2,1,0:T(8,128)(2,1)} %query_ref.1, bf16[3,128,1024]{2,1,0:T(8,128)(2,1)} %key_ref.1, bf16[3,128,1024]{2,1,0:T(8,128)(2,1)} %value_ref.1, f32[3,2,128]{2,1,0:T(2,128)} %bitcast.1, bf16[2,32,512]{2,1,0:T(8,128)(2,1)} %first_ref.1, bf16[2,32,512]{2,1,0:T(8,128)(2,1)} %third_ref.1, ...), custom_call_target="tpu_custom_call" | custom-call | tf_op jit(solution)/shard_map/pallas_call | solution.py:502
  70.9 0.9 %copy.10 = bf16[3,128,1024]{2,1,0:T(8,128)(2,1)} copy(bf16[3,128,1024]{2,1,0:T(8,128)(2,1)S(1)} %shard_map.82) | data formatting | bytes 1572864

commit v3 on v2

--- a/solution.py
+++ b/solution.py
@@ -131,6 +131,8 @@
     rows_here,
     sum_send,
     sum_recv,
+    side_send,
+    side_recv,
     out_send,
     out_recv,
     out_local,
@@ -208,7 +210,7 @@
     def block_of(k, m, p, q):
         return full.at[k, m, p, :, q, core]
 
-    def gather_copy(k, m, n):
+    def gather_copy(k, m, n, h):
         p, q = (
             (pair, lane),
             (pair, lane),
@@ -218,9 +220,11 @@
             (pair, 1 - lane),
             (1 - pair, 1 - lane),
         )[n]
-        span = block_of(k, m, p, q)
+        span = full.at[k, m, p, h, q, core]
         to = (beyond, beside, beside, partner, partner, partner, partner)[n]
-        return push(span, span, gather_send.at[k - 1, m, n], gather_recv.at[k - 1, m, n], to)
+        return push(
+            span, span, gather_send.at[k - 1, m, n, h], gather_recv.at[k - 1, m, n, h], to
+        )
 
     share = pl.ds(pl.multiple_of(group * (width // 2), width // 2), width // 2)
 
@@ -289,65 +293,76 @@
         for n in (4, 11, 12, 13, 14):
             first_copy(m, n).wait_recv()
 
-    def gather_own(k, m):
+    def gather_own(k, m, h):
         for n in (0, 1, 3):
-            go(gather_copy(k, m, n))
+            go(gather_copy(k, m, n, h))
 
     def gather_beyond(k, m):
-        gather_copy(k, m, 0).wait_recv()
-        go(gather_copy(k, m, 2))
-        go(gather_copy(k, m, 4))
+        for h in range(2):
+            gather_copy(k, m, 0, h).wait_recv()
+            go(gather_copy(k, m, 2, h))
+            go(gather_copy(k, m, 4, h))
 
     def gather_beside(k, m, n):
-        gather_copy(k, m, n).wait_recv()
-        go(gather_copy(k, m, n + 4))
+        for h in range(2):
+            gather_copy(k, m, n, h).wait_recv()
+            go(gather_copy(k, m, n + 4, h))
 
     def gather_end(k, m):
         for n in range(3, 7):
-            gather_copy(k, m, n).wait_recv()
+            for h in range(2):
+                gather_copy(k, m, n, h).wait_recv()
 
     def core_copy(t):
         return push(
-            core_out.at[t], core_in.at[t], sum_send.at[t, 0], sum_recv.at[t, 0], partner
-        )
-
-    def side_copy(t, p, n):
+            core_out.at[t], core_in.at[t], sum_send.at[t], sum_recv.at[t], partner
+        )
+
+    def side_copy(t, p, n, h):
         return push(
-            side_out.at[t, p], side_in.at[t, p], sum_send.at[t, n], sum_recv.at[t, n], beside
-        )
-
-    def far_copy(t):
-        return push(far_out.at[t], far_in.at[t], sum_send.at[t, 3], sum_recv.at[t, 3], beyond)
+            side_out.at[t, p, h],
+            side_in.at[t, p, h],
+            side_send.at[t, n, h],
+            side_recv.at[t, n, h],
+            beside,
+        )
+
+    def far_copy(t, h):
+        return push(
+            far_out.at[t, h], far_in.at[t, h], side_send.at[t, 2, h], side_recv.at[t, 2, h], beyond
+        )
 
     def core_start(t):
         core_out[t] = part[t, :, :, :, 1 - core].astype(jnp.bfloat16)
         go(core_copy(t))
 
-    def core_sum(t, p, q):
-        return part[t, p, :, q, core] + core_in[t, p, :, q].astype(jnp.float32)
+    def core_sum(t, p, q, h):
+        return part[t, p, h, q, core] + core_in[t, p, h, q].astype(jnp.float32)
 
     def side_start(ts):
-        for n in (1, 2):
+        for n in (0, 1):
             for t in ts:
-                if n == 1:
+                if n == 0:
                     core_copy(t).wait_recv()
-                p = 1 - pair if n == 1 else pair
-                side_out[t, p] = core_sum(t, p, 1 - lane).astype(jnp.bfloat16)
-                go(side_copy(t, p, n))
+                p = 1 - pair if n == 0 else pair
+                for h in range(2):
+                    side_out[t, p, h] = core_sum(t, p, 1 - lane, h).astype(jnp.bfloat16)
+                    go(side_copy(t, p, n, h))
 
     def far_start(t):
         p = 1 - pair
-        side_copy(t, p, 1).wait_recv()
-        far_out[t] = (core_sum(t, p, lane) + side_in[t, p].astype(jnp.float32)).astype(
-            jnp.bfloat16
-        )
-        go(far_copy(t))
-
-    def total_of(t):
-        side_copy(t, pair, 2).wait_recv()
-        near = core_sum(t, pair, lane) + side_in[t, pair].astype(jnp.float32)
-        far_copy(t).wait_recv()
-        return near + far_in[t].astype(jnp.float32)
+        for h in range(2):
+            side_copy(t, p, 0, h).wait_recv()
+            far_out[t, h] = (
+                core_sum(t, p, lane, h) + side_in[t, p, h].astype(jnp.float32)
+            ).astype(jnp.bfloat16)
+            go(far_copy(t, h))
+
+    def total_of(t, h):
+        side_copy(t, pair, 1, h).wait_recv()
+        near = core_sum(t, pair, lane, h) + side_in[t, pair, h].astype(jnp.float32)
+        far_copy(t, h).wait_recv()
+        return near + far_in[t, h].astype(jnp.float32)
 
     order = (2, 0, 1)
 
@@ -430,16 +445,17 @@
     steps(1)
     for m in order:
         far_start(m)
-    side_start([3 + m for m in order])
+        side_start([3 + m])
     swap(6, 7)
     for m in order:
-        moment = total_of(m)
-        step_own[m] = moment
-        old = full[0, m, pair, :, lane, core].astype(jnp.float32)
-        fresh = renorm(old, old + moment)
-        weight_own[m] = fresh
-        full[1, m, pair, :, lane, core] = fresh.astype(jnp.bfloat16)
-        gather_own(1, m)
+        for h in range(2):
+            moment = total_of(m, h)
+            step_own[m, h] = moment
+            old = full[0, m, pair, h, lane, core].astype(jnp.float32)
+            fresh = renorm(old, old + moment)
+            weight_own[m, h] = fresh
+            full[1, m, pair, h, lane, core] = fresh.astype(jnp.bfloat16)
+            gather_own(1, m, h)
     decay = decay_ref[head]
     for m in order:
         far_start(3 + m)
@@ -451,11 +467,12 @@
     read_hidden(0)
     read_out(0)
     for m in order:
-        moment = decay * step_own[m] + total_of(3 + m)
-        old = weight_own[m]
-        fresh = renorm(old, old + moment)
-        full[2, m, pair, :, lane, core] = fresh.astype(jnp.bfloat16)
-        gather_own(2, m)
+        for h in range(2):
+            moment = decay * step_own[m, h] + total_of(3 + m, h)
+            old = weight_own[m, h]
+            fresh = renorm(old, old + moment)
+            full[2, m, pair, h, lane, core] = fresh.astype(jnp.bfloat16)
+            gather_own(2, m, h)
     swap(8, 9)
     for m in order:
         gather_beside(1, m, 2)
@@ -526,14 +543,16 @@
             dma((9,)),
             dma((9,)),
             dma((9,)),
-            dma((2, 3, 7)),
-            dma((2, 3, 7)),
+            dma((2, 3, 7, 2)),
+            dma((2, 3, 7, 2)),
             dma((3, 15)),
             dma((3, 15)),
             dma((3,)),
             pltpu.VMEM((3, heads, rows, width), low),
-            dma((6, 4)),
-            dma((6, 4)),
+            dma((6,)),
+            dma((6,)),
+            dma((6, 3, 2)),
+            dma((6, 3, 2)),
             dma((3,)),
             dma((3,)),
             dma((3,)),

time: 71.9 us -> 70.9 us (0.986)
  Pallas kernels: 70.9 us -> 69.8 us
    pallas_call x1, Pallas kernels: 70.9 us -> 69.8 us  [fused_shards(): pl.pallas_call(kernel, out_shape=pltpu.VMEM(query.shape, low), in_specs=[...]
where the time goes in v3:
time: 70.9 us; the launch traced here: 70.7 us
  Pallas kernels  69.8 us (98%)
  local copies, waits for them, and re-layouts  0.88 us (1%)
    pallas_call x1, Pallas kernels, fused_shards(): pl.pallas_call(kernel, out_shape=pltpu.VMEM(query.shape, low), in_specs=[...  69.8 us

profile of v3, /device:TPU:0, one launch (start us, length us, event | category | flops | bytes accessed | tf_op | source)
XLA Modules:
  0.0 70.7 jit_solution(10199467260436385688)
XLA Ops:
  0.0 69.8 %shard_map.82 = bf16[3,128,1024]{2,1,0:T(8,128)(2,1)S(1)} custom-call(bf16[3,128,1024]{2,1,0:T(8,128)(2,1)} %query_ref.1, bf16[3,128,1024]{2,1,0:T(8,128)(2,1)} %key_ref.1, bf16[3,128,1024]{2,1,0:T(8,128)(2,1)} %value_ref.1, f32[3,2,128]{2,1,0:T(2,128)} %bitcast.1, bf16[2,32,512]{2,1,0:T(8,128)(2,1)} %first_ref.1, bf16[2,32,512]{2,1,0:T(8,128)(2,1)} %third_ref.1, ...), custom_call_target="tpu_custom_call" | custom-call | tf_op jit(solution)/shard_map/pallas_call | solution.py:519
  69.8 0.9 %copy.10 = bf16[3,128,1024]{2,1,0:T(8,128)(2,1)} copy(bf16[3,128,1024]{2,1,0:T(8,128)(2,1)S(1)} %shard_map.82) | data formatting | bytes 1572864

commit v4 on v3

--- a/solution.py
+++ b/solution.py
@@ -275,6 +275,7 @@
             first_copy(m, 1).wait_recv()
             for n in (7, 9, 8):
                 go(first_copy(m, n))
+        swap(3, 6)
         for m in range(3):
             first_copy(m, 6).wait_recv()
             go(first_copy(m, 11))
@@ -339,15 +340,18 @@
     def core_sum(t, p, q, h):
         return part[t, p, h, q, core] + core_in[t, p, h, q].astype(jnp.float32)
 
+    def side_piece(t, n):
+        if n == 0:
+            core_copy(t).wait_recv()
+        p = 1 - pair if n == 0 else pair
+        for h in range(2):
+            side_out[t, p, h] = core_sum(t, p, 1 - lane, h).astype(jnp.bfloat16)
+            go(side_copy(t, p, n, h))
+
     def side_start(ts):
         for n in (0, 1):
             for t in ts:
-                if n == 0:
-                    core_copy(t).wait_recv()
-                p = 1 - pair if n == 0 else pair
-                for h in range(2):
-                    side_out[t, p, h] = core_sum(t, p, 1 - lane, h).astype(jnp.bfloat16)
-                    go(side_copy(t, p, n, h))
+                side_piece(t, n)
 
     def far_start(t):
         p = 1 - pair
@@ -430,7 +434,7 @@
         outs.append(here)
 
     first_start()
-    swap(0, 6)
+    swap(0, 3)
     first_spread()
     for m in range(2):
         first_end(m)
@@ -439,13 +443,16 @@
     keys_forward(0)
     steps(0)
     side_start(order)
+    for m in order:
+        far_start(m)
     for n in range(3, 6):
         ready(n)
     keys_forward(1)
     steps(1)
     for m in order:
-        far_start(m)
-        side_start([3 + m])
+        side_piece(3 + m, 0)
+    for m in order:
+        side_piece(3 + m, 1)
     swap(6, 7)
     for m in order:
         for h in range(2):
@@ -457,7 +464,8 @@
             full[1, m, pair, h, lane, core] = fresh.astype(jnp.bfloat16)
             gather_own(1, m, h)
     decay = decay_ref[head]
-    for m in order:
+    last = (0, 1, 2)
+    for m in last:
         far_start(3 + m)
     swap(7, 8)
     for m in order:
@@ -466,7 +474,7 @@
     ready(6)
     read_hidden(0)
     read_out(0)
-    for m in order:
+    for m in last:
         for h in range(2):
             moment = decay * step_own[m, h] + total_of(3 + m, h)
             old = weight_own[m, h]
@@ -476,7 +484,7 @@
     swap(8, 9)
     for m in order:
         gather_beside(1, m, 2)
-    for m in order:
+    for m in last:
         gather_beyond(2, m)
         gather_beside(2, m, 1)
     for m in range(3):
@@ -485,19 +493,35 @@
     read_hidden(1)
     read_out(1)
     ready(8)
-    for m in order:
+    for m in range(2):
         gather_beside(2, m, 2)
-    gather_end(2, 2)
-    gather_end(2, 0)
-    gates[...] = dot_nt(queries[2], whole(2, 0))
-    gather_end(2, 1)
-    for place in (other_slot, slot):
-        gate = gates[place, :]
-        up = dot_nt(queries[2, place, :], whole(2, 1))
-        hidden = (gate * jax.nn.sigmoid(gate) * up).astype(jnp.bfloat16)
-        result[2, place, :] = dot_nt(hidden, whole(2, 2)).astype(jnp.bfloat16)
-        if place is other_slot:
-            send_out(2)
+    for m in range(2):
+        gather_end(2, m)
+    gate, up, sig, hidden = forward(2, queries[2])
+    hiddens[...] = hidden
+    for n in (3, 5):
+        for h in range(2):
+            gather_copy(2, 2, n, h).wait_recv()
+    columns = width // 2
+    for n, p in enumerate((pair, 1 - pair)):
+        if n == 1:
+            gather_beside(2, 2, 2)
+            for e in (4, 6):
+                for h in range(2):
+                    gather_copy(2, 2, e, h).wait_recv()
+        some = pl.ds(pl.multiple_of(p * columns, columns), columns)
+        down = full[2, 2, p].reshape(columns, width)
+        result[2, :, some] = dot_nt(hiddens[...], down).astype(jnp.bfloat16)
+        place = pl.ds(pl.multiple_of(head * width + p * columns, columns), columns)
+        away = push(
+            result.at[2, other_slot, some],
+            out_ref.at[2, :, place],
+            out_send.at[2 + n],
+            out_recv.at[2 + n],
+            mate,
+        )
+        away.start()
+        outs.append(away)
     keep_out(2)
 
     for n in range(len(pairs)):
@@ -553,8 +577,8 @@
             dma((6,)),
             dma((6, 3, 2)),
             dma((6, 3, 2)),
-            dma((3,)),
-            dma((3,)),
+            dma((4,)),
+            dma((4,)),
             dma((3,)),
         ],
         compiler_params=pltpu.CompilerParams(

time: 70.9 us -> 69.4 us (0.979)
  Pallas kernels: 69.8 us -> 68.4 us
    pallas_call x1, Pallas kernels: 69.8 us -> 68.4 us  [fused_shards(): pl.pallas_call(kernel, out_shape=pltpu.VMEM(query.shape, low), in_specs=[...]
where the time goes in v4:
time: 69.4 us; the launch traced here: 69.3 us
  Pallas kernels  68.4 us (99%)
  local copies, waits for them, and re-layouts  0.88 us (1%)
    pallas_call x1, Pallas kernels, fused_shards(): pl.pallas_call(kernel, out_shape=pltpu.VMEM(query.shape, low), in_specs=[...  68.4 us

profile of v4, /device:TPU:0, one launch (start us, length us, event | category | flops | bytes accessed | tf_op | source)
XLA Modules:
  0.0 69.3 jit_solution(14137138620504969779)
XLA Ops:
  0.0 68.4 %shard_map.82 = bf16[3,128,1024]{2,1,0:T(8,128)(2,1)S(1)} custom-call(bf16[3,128,1024]{2,1,0:T(8,128)(2,1)} %query_ref.1, bf16[3,128,1024]{2,1,0:T(8,128)(2,1)} %key_ref.1, bf16[3,128,1024]{2,1,0:T(8,128)(2,1)} %value_ref.1, f32[3,2,128]{2,1,0:T(2,128)} %bitcast.1, bf16[2,32,512]{2,1,0:T(8,128)(2,1)} %first_ref.1, bf16[2,32,512]{2,1,0:T(8,128)(2,1)} %third_ref.1, ...), custom_call_target="tpu_custom_call" | custom-call | tf_op jit(solution)/shard_map/pallas_call | solution.py:543
  68.4 0.9 %copy.10 = bf16[3,128,1024]{2,1,0:T(8,128)(2,1)} copy(bf16[3,128,1024]{2,1,0:T(8,128)(2,1)S(1)} %shard_map.82) | data formatting | bytes 1572864

commit v5 on v4

--- a/solution.py
+++ b/solution.py
@@ -221,6 +221,9 @@
             (1 - pair, 1 - lane),
         )[n]
         span = full.at[k, m, p, h, q, core]
+        if (k, m) == (2, 2):
+            part_rows = slice(h % 2 * (rows // 2), (h % 2 + 1) * (rows // 2))
+            span = full.at[k, m, p, h // 2, q, core, part_rows, :]
         to = (beyond, beside, beside, partner, partner, partner, partner)[n]
         return push(
             span, span, gather_send.at[k - 1, m, n, h], gather_recv.at[k - 1, m, n, h], to
@@ -294,24 +297,27 @@
         for n in (4, 11, 12, 13, 14):
             first_copy(m, n).wait_recv()
 
+    def pieces(k, m):
+        return range(4 if (k, m) == (2, 2) else 2)
+
     def gather_own(k, m, h):
         for n in (0, 1, 3):
             go(gather_copy(k, m, n, h))
 
     def gather_beyond(k, m):
-        for h in range(2):
+        for h in pieces(k, m):
             gather_copy(k, m, 0, h).wait_recv()
             go(gather_copy(k, m, 2, h))
             go(gather_copy(k, m, 4, h))
 
     def gather_beside(k, m, n):
-        for h in range(2):
+        for h in pieces(k, m):
             gather_copy(k, m, n, h).wait_recv()
             go(gather_copy(k, m, n + 4, h))
 
     def gather_end(k, m):
         for n in range(3, 7):
-            for h in range(2):
+            for h in pieces(k, m):
                 gather_copy(k, m, n, h).wait_recv()
 
     def core_copy(t):
@@ -453,7 +459,7 @@
         side_piece(3 + m, 0)
     for m in order:
         side_piece(3 + m, 1)
-    swap(6, 7)
+    swap(6, 8)
     for m in order:
         for h in range(2):
             moment = total_of(m, h)
@@ -467,7 +473,6 @@
     last = (0, 1, 2)
     for m in last:
         far_start(3 + m)
-    swap(7, 8)
     for m in order:
         gather_beyond(1, m)
         gather_beside(1, m, 1)
@@ -480,7 +485,8 @@
             old = weight_own[m, h]
             fresh = renorm(old, old + moment)
             full[2, m, pair, h, lane, core] = fresh.astype(jnp.bfloat16)
-            gather_own(2, m, h)
+            for piece in (2 * h, 2 * h + 1) if m == 2 else (h,):
+                gather_own(2, m, piece)
     swap(8, 9)
     for m in order:
         gather_beside(1, m, 2)
@@ -500,14 +506,14 @@
     gate, up, sig, hidden = forward(2, queries[2])
     hiddens[...] = hidden
     for n in (3, 5):
-        for h in range(2):
+        for h in pieces(2, 2):
             gather_copy(2, 2, n, h).wait_recv()
     columns = width // 2
     for n, p in enumerate((pair, 1 - pair)):
         if n == 1:
             gather_beside(2, 2, 2)
             for e in (4, 6):
-                for h in range(2):
+                for h in pieces(2, 2):
                     gather_copy(2, 2, e, h).wait_recv()
         some = pl.ds(pl.multiple_of(p * columns, columns), columns)
         down = full[2, 2, p].reshape(columns, width)
@@ -567,8 +573,8 @@
             dma((9,)),
             dma((9,)),
             dma((9,)),
-            dma((2, 3, 7, 2)),
-            dma((2, 3, 7, 2)),
+            dma((2, 3, 7, 4)),
+            dma((2, 3, 7, 4)),
             dma((3, 15)),
             dma((3, 15)),
             dma((3,)),

time: 69.4 us -> 71 us (1.023)
  Pallas kernels: 68.4 us -> 69.9 us
    pallas_call x1, Pallas kernels: 68.4 us -> 69.9 us  [fused_shards(): pl.pallas_call(kernel, out_shape=pltpu.VMEM(query.shape, low), in_specs=[...]
where the time goes in v5:
time: 71 us; the launch traced here: 70.8 us
  Pallas kernels  69.9 us (98%)
  local copies, waits for them, and re-layouts  0.88 us (1%)
    pallas_call x1, Pallas kernels, fused_shards(): pl.pallas_call(kernel, out_shape=pltpu.VMEM(query.shape, low), in_specs=[...  69.9 us

profile of v5, /device:TPU:0, one launch (start us, length us, event | category | flops | bytes accessed | tf_op | source)
XLA Modules:
  0.0 70.8 jit_solution(11793406450797995322)
XLA Ops:
  0.0 69.9 %shard_map.82 = bf16[3,128,1024]{2,1,0:T(8,128)(2,1)S(1)} custom-call(bf16[3,128,1024]{2,1,0:T(8,128)(2,1)} %query_ref.1, bf16[3,128,1024]{2,1,0:T(8,128)(2,1)} %key_ref.1, bf16[3,128,1024]{2,1,0:T(8,128)(2,1)} %value_ref.1, f32[3,2,128]{2,1,0:T(2,128)} %bitcast.1, bf16[2,32,512]{2,1,0:T(8,128)(2,1)} %first_ref.1, bf16[2,32,512]{2,1,0:T(8,128)(2,1)} %third_ref.1, ...), custom_call_target="tpu_custom_call" | custom-call | tf_op jit(solution)/shard_map/pallas_call | solution.py:549
  70.0 0.9 %copy.10 = bf16[3,128,1024]{2,1,0:T(8,128)(2,1)} copy(bf16[3,128,1024]{2,1,0:T(8,128)(2,1)S(1)} %shard_map.82) | data formatting | bytes 1572864

commit v6 on v4

--- a/solution.py
+++ b/solution.py
@@ -275,7 +275,6 @@
             first_copy(m, 1).wait_recv()
             for n in (7, 9, 8):
                 go(first_copy(m, n))
-        swap(3, 6)
         for m in range(3):
             first_copy(m, 6).wait_recv()
             go(first_copy(m, 11))
@@ -436,6 +435,7 @@
     first_start()
     swap(0, 3)
     first_spread()
+    swap(3, 6)
     for m in range(2):
         first_end(m)
     for n in range(0, 3):
@@ -453,7 +453,7 @@
         side_piece(3 + m, 0)
     for m in order:
         side_piece(3 + m, 1)
-    swap(6, 7)
+    swap(6, 8)
     for m in order:
         for h in range(2):
             moment = total_of(m, h)
@@ -467,7 +467,6 @@
     last = (0, 1, 2)
     for m in last:
         far_start(3 + m)
-    swap(7, 8)
     for m in order:
         gather_beyond(1, m)
         gather_beside(1, m, 1)

time: 69.4 us -> 69 us (level)
  no operation moved by 1% of the time
where the time goes in v6:
time: 69 us; the launch traced here: 68.8 us
  Pallas kernels  67.9 us (98%)
  local copies, waits for them, and re-layouts  0.88 us (1%)
    pallas_call x1, Pallas kernels, fused_shards(): pl.pallas_call(kernel, out_shape=pltpu.VMEM(query.shape, low), in_specs=[...  67.9 us

profile of v6, /device:TPU:0, one launch (start us, length us, event | category | flops | bytes accessed | tf_op | source)
XLA Modules:
  0.0 68.8 jit_solution(15119962541053875737)
XLA Ops:
  0.0 67.9 %shard_map.82 = bf16[3,128,1024]{2,1,0:T(8,128)(2,1)S(1)} custom-call(bf16[3,128,1024]{2,1,0:T(8,128)(2,1)} %query_ref.1, bf16[3,128,1024]{2,1,0:T(8,128)(2,1)} %key_ref.1, bf16[3,128,1024]{2,1,0:T(8,128)(2,1)} %value_ref.1, f32[3,2,128]{2,1,0:T(2,128)} %bitcast.1, bf16[2,32,512]{2,1,0:T(8,128)(2,1)} %first_ref.1, bf16[2,32,512]{2,1,0:T(8,128)(2,1)} %third_ref.1, ...), custom_call_target="tpu_custom_call" | custom-call | tf_op jit(solution)/shard_map/pallas_call | solution.py:542
  67.9 0.9 %copy.10 = bf16[3,128,1024]{2,1,0:T(8,128)(2,1)} copy(bf16[3,128,1024]{2,1,0:T(8,128)(2,1)S(1)} %shard_map.82) | data formatting | bytes 1572864
